TPU v7x, 32 devices: a whole 2x2x4 slice. The times are simulated.
32 devices in a mesh: dp: 8 (over z, x), pipe: 4 (over y, core).
Axes of the slice: x: 2, y: 2, z: 4, core: 2. Of those that a mesh axis runs over, the one named last changes fastest.
Arguments:
- noise_draw: bfloat16 [2, 14976, 128], P(None, 'dp'), may hold values from -6 to 6
- single_step: bfloat16 [2, 14976, 128], P(None, 'dp'), may hold values from -6 to 6
- double_step: bfloat16 [2, 14976, 128], P(None, 'dp'), may hold values from -6 to 6
- state_now: bfloat16 [2, 14976, 128], P(None, 'dp'), may hold values from -6 to 6
- target_flag: int32 [2, 8], P(None, 'dp'), may hold values from 0 to 1
- flow_time: float32 [2, 8], P(None, 'dp'), may hold values from 0.05 to 0.95
- live_count: int32 [2, 8], P(None, 'dp'), may hold values from 507 to 1872, as said below
- latitude_row: int32 [2, 1152], P(None, 'dp'), may hold values from 0 to 59
- window_order: int32 [2, 14976], P(None, 'dp'), may hold values from 0 to 1871, as said below
- latitude_weight: int32 [60], replicated, may hold values from 100 to 1000
- level_weight: int32 [13], replicated, may hold values from 100 to 1000
- step_count: int32 [1], replicated, may hold values from 2 to 20
- master_weights: float32 [6528, 384], P('dp')
- first_moment: float32 [6528, 384], P('dp')
- second_moment: float32 [6528, 384], P('dp')
- average_weights: float32 [6528, 384], P('dp')
- gain_rows: float32 [5, 384], replicated
- gain_first: float32 [5, 384], replicated
- gain_second: float32 [5, 384], replicated
- gain_average: float32 [5, 384], replicated
Outputs:
- loss_value: float32 [], replicated
- grad_norm: float32 [], replicated
- new_weights: float32 [6528, 384], P('dp')
- new_first: float32 [6528, 384], P('dp')
- new_second: float32 [6528, 384], P('dp')
- new_average: float32 [6528, 384], P('dp')
- weights_low: bfloat16 [6528, 384], P('dp')
- new_gains: float32 [5, 384], replicated
- new_gain_first: float32 [5, 384], replicated
- new_gain_second: float32 [5, 384], replicated
- new_gain_average: float32 [5, 384], replicated
Inputs may be any that keep to these rules, and one draw needn't show every extreme that they name: `window_order`: each index of dp and micro-batch holds its own block of 1872 entries, a permutation of 0 to 1871 naming the block's own patches. `live_count`: the first that many patches of a block count; it rises along dp, and the last index of dp holds 1872 in every micro-batch.
All inputs are finite; a program needn't handle non-finite values.
Results may differ from a plain program's by a relative error of at most 0.0038.
Values may be sent and summed in bfloat16 or wider, within the bound.
A program may use at most 256 MiB of HBM per device.

v0:
```python
import functools
from types import SimpleNamespace

import jax
import jax.numpy as jnp
import numpy as np
from jax import lax
from jax.experimental import pallas as pl
from jax.experimental.pallas import tpu as pltpu
from jax.sharding import PartitionSpec as P

D = 384
HEADS = 12
HD = 32
FF = 1536
PIN = 128
LEV = 13
WSZ = 144
LATN = 60

EPS_NORM = 1e-05
CLIP_MAX = 0.01
RATE = 0.03
GAIN_RATE = 0.3
BETA = 0.5
EPS_ADAM = 1e-08
DECAY_WEIGHT = 0.05
EMA_RATE = 0.8

F32 = jnp.float32
BF16 = jnp.bfloat16
MESH = pl.DeviceIdType.MESH

SOFT = HD ** (-0.5) * 1.4426950408889634
GROUPS = 3
PACK = 4
LANES = 128

ROWS = 1008
TILE = 336
TILES = 3
WINS = 7
CHUNKS = 9
CROWS = 112
TAIL = WSZ - LANES
SKEW = (3, 6)
VMEM_MAX = 63 * 2**20


def block_starts():
    widths = [2 * PIN, 3 * D, D, FF, FF, 3 * D, D, PIN]
    starts = [0]
    for width in widths:
        starts.append(starts[-1] + width)
    return starts


STARTS = block_starts()


def natural_order(stored, pieces_count):
    view = stored.reshape(pieces_count, stored.shape[0] // pieces_count, stored.shape[1])
    pieces = []
    for number in range(8):
        pieces.append(
            view[:, STARTS[number] // pieces_count : STARTS[number + 1] // pieces_count].reshape(
                -1, stored.shape[1]
            )
        )
    return jnp.concatenate(pieces, axis=0)


def stored_order(natural, pieces_count):
    pieces = []
    for number in range(8):
        pieces.append(
            natural[STARTS[number] : STARTS[number + 1]].reshape(pieces_count, -1, natural.shape[1])
        )
    return jnp.concatenate(pieces, axis=1).reshape(-1, natural.shape[1])


def dot(left, right):
    return jnp.dot(left, right, preferred_element_type=F32)


def dot_nt(left, right):
    return lax.dot_general(left, right, (((1,), (1,)), ((), ())), preferred_element_type=F32)


def dot_tn(left, right):
    return lax.dot_general(left, right, (((0,), (0,)), ((), ())), preferred_element_type=F32)


def standardize(values):
    center = values - jnp.mean(values, axis=-1, keepdims=True)
    spread = lax.rsqrt(jnp.mean(center * center, axis=-1, keepdims=True) + EPS_NORM)
    return center * spread, spread


def standardize_back(scaled, spread, gain, upstream):
    inner = upstream * gain
    return spread * (
        inner
        - jnp.mean(inner, axis=-1, keepdims=True)
        - scaled * jnp.mean(inner * scaled, axis=-1, keepdims=True)
    )


def head_masks(dtype):
    lane = lax.broadcasted_iota(jnp.int32, (1, LANES), 1) // HD
    return [jnp.where(lane == h, 1.0, 0.0).astype(dtype) for h in range(PACK)]


def group_at(which, g):
    start = which * D + g * LANES
    return slice(start, start + LANES)


def staged(count, between, *stages):
    for i in range(count + SKEW[-1]):
        for shift, stage in zip((0, *SKEW), stages):
            if 0 <= i - shift < count:
                stage(i - shift)
        if i in between:
            between[i]()


def soft_columns(scores):
    top = jnp.max(scores, axis=0, keepdims=True)
    expo = jnp.exp2((scores - top) * SOFT)
    return (expo * (1.0 / jnp.sum(expo, axis=0, keepdims=True))).astype(BF16)


def spread_padded(block):
    n = block.shape[0]
    parts = []
    for mask in head_masks(block.dtype):
        parts.append(block * mask)
        if n < LANES:
            parts.append(jnp.zeros((LANES - n, LANES), block.dtype))
    return jnp.concatenate(parts, axis=0)


def head_lanes(i):
    return slice(i * LANES, (i + 1) * LANES)


def attend_heads(units, bias, between):
    scores, probs = {}, {}

    def score(i):
        queries, keys = units[i][:2]
        scores[i] = dot_nt(keys, spread_padded(queries))

    def soften(i):
        value = scores.pop(i)
        parts = []
        for h in range(PACK):
            part = value[:, head_lanes(h)]
            parts.append(soft_columns(part if bias is None else part + bias))
            units[i][3](h, parts[h])
        probs[i] = parts

    def mix(i):
        flipped = jnp.transpose(units[i][2])
        parts = probs.pop(i)
        context = [dot(flipped[h * HD : (h + 1) * HD, :], parts[h]) for h in range(PACK)]
        units[i][4](jnp.transpose(jnp.concatenate(context, axis=0)))

    staged(len(units), between, score, soften, mix)


def attend_heads_back(units, between):
    factor = HD ** (-0.5)
    slopes, lows, ups = {}, {}, {}

    def slope(i):
        ups[i] = spread_padded(units[i][3])
        slopes[i] = dot_nt(units[i][2], ups[i])

    def soften(i):
        given, parts = slopes.pop(i), []
        for h in range(PACK):
            part = given[:, head_lanes(h)]
            wide = units[i][4](h).astype(F32)
            delta = jnp.sum(wide * part, axis=0, keepdims=True)
            parts.append((wide * (part - delta)).astype(BF16))
        lows[i] = parts

    def mix(i):
        queries, keys = units[i][:2]
        parts = lows.pop(i)
        flipped = jnp.transpose(keys)
        to_query = [dot(flipped[h * HD : (h + 1) * HD, :], parts[h]) for h in range(PACK)]
        to_query = jnp.transpose(jnp.concatenate(to_query, axis=0))
        to_key = dot(jnp.concatenate(parts, axis=1), spread_padded(queries))
        chances = jnp.concatenate([units[i][4](h) for h in range(PACK)], axis=1)
        to_value = dot(chances, ups.pop(i))
        units[i][5](to_query * factor, to_key * factor, to_value)

    staged(len(units), between, slope, soften, mix)


def all_masks(dtype):
    lane = lax.broadcasted_iota(jnp.int32, (1, D), 1) // HD
    return [jnp.where(lane == h, 1.0, 0.0).astype(dtype) for h in range(HEADS)]


def spread_all(block):
    return jnp.concatenate([block * mask for mask in all_masks(block.dtype)], axis=0)


def gather_all(stacked):
    total = None
    for h, mask in enumerate(all_masks(F32)):
        part = stacked[h * TAIL : (h + 1) * TAIL] * mask
        total = part if total is None else total + part
    return total


def attend_windows(packed, spots, probs, probs_tail, context, between):
    units, lows = [], []
    for w, rows_main, rows_tail, rows in spots:
        low = soft_columns(dot_nt(packed[rows, D : 2 * D], spread_all(packed[rows_tail, 0:D])))
        probs_tail[w] = low
        lows.append(low)

        def unit(g, w=w, rows_main=rows_main, rows=rows):
            def keep_probs(h, value):
                probs[w, :, head_lanes(g * PACK + h)] = value

            def keep_context(value):
                context[rows_main, head_lanes(g)] = value.astype(BF16)

            return (
                packed[rows_main, group_at(0, g)],
                packed[rows, group_at(1, g)],
                packed[rows, group_at(2, g)],
                keep_probs,
                keep_context,
            )

        units += [unit(g) for g in range(GROUPS)]
    attend_heads(units, None, between)
    for (w, rows_main, rows_tail, rows), low in zip(spots, lows):
        mixed = gather_all(dot_tn(low, packed[rows, 2 * D :]))
        context[rows_tail, :] = mixed.astype(BF16)


def attend_windows_back(packed, spots, probs, probs_tail, upstream, between):
    factor = HD ** (-0.5)
    units, queries = [], []
    for w, rows_main, rows_tail, rows in spots:
        low = probs_tail[w]
        wide = low.astype(F32)
        spread_up = spread_all(upstream[rows_tail, :])
        given = dot_nt(packed[rows, 2 * D :], spread_up)
        delta = jnp.sum(wide * given, axis=0, keepdims=True)
        slope = (wide * (given - delta)).astype(BF16)
        queries.append(gather_all(dot_tn(slope, packed[rows, D : 2 * D])) * factor)
        tail_key = dot(slope, spread_all(packed[rows_tail, 0:D])) * factor
        tail_value = dot(low, spread_up)

        def unit(g, w=w, rows_main=rows_main, rows=rows, tail_key=tail_key, tail_value=tail_value):
            part = head_lanes(g)

            def keep(to_query, to_key, to_value):
                packed[rows_main, group_at(0, g)] = to_query.astype(BF16)
                packed[rows, group_at(1, g)] = (to_key + tail_key[:, part]).astype(BF16)
                packed[rows, group_at(2, g)] = (to_value + tail_value[:, part]).astype(BF16)

            return (
                packed[rows_main, group_at(0, g)],
                packed[rows, group_at(1, g)],
                packed[rows, group_at(2, g)],
                upstream[rows_main, part],
                lambda h: probs[w, :, head_lanes(g * PACK + h)],
                keep,
            )

        units += [unit(g) for g in range(GROUPS)]
    attend_heads_back(units, between)
    for (w, rows_main, rows_tail, rows), query in zip(spots, queries):
        packed[rows_tail, 0:D] = query.astype(BF16)


def attend_columns(packed, chunks, probs, bias, context):
    def unit(rows, g):
        def keep_probs(h, value):
            probs[rows, head_lanes(g * PACK + h)] = value

        def keep_context(value):
            context[rows, head_lanes(g)] = value[:CROWS].astype(BF16)

        return (*(packed[rows, group_at(i, g)] for i in range(3)), keep_probs, keep_context)

    attend_heads([unit(rows, g) for rows in chunks for g in range(GROUPS)], bias, {})


def attend_columns_back(packed, chunks, probs, upstream):
    def unit(rows, g):
        def keep(to_query, to_key, to_value):
            packed[rows, group_at(0, g)] = to_query[:CROWS].astype(BF16)
            packed[rows, group_at(1, g)] = to_key.astype(BF16)
            packed[rows, group_at(2, g)] = to_value.astype(BF16)

        return (
            *(packed[rows, group_at(i, g)] for i in range(3)),
            upstream[rows, head_lanes(g)],
            lambda h: probs[rows, head_lanes(g * PACK + h)],
            keep,
        )

    attend_heads_back([unit(rows, g) for rows in chunks for g in range(GROUPS)], {})


def column_of(row):
    wide = jnp.broadcast_to(row.astype(F32), (LANES, row.shape[1]))
    return jnp.transpose(wide)


def tile_at(t):
    return pl.ds(pl.multiple_of(t * TILE, 16), TILE)


WIDTHS = (2 * PIN, 3 * D, D, FF, FF, 3 * D, D, PIN)
NAMES = ("E", "A1", "O1", "U", "V", "A2", "O2", "Q")
PACKED = dict(E=0, A1=48, O1=192, Q=240, U=256, V=448, A2=640, O2=784)
SPARE = slice(32, 48)
PACKED_ROWS = 832
SHARDS = 8
GATHERS = (
    (0, 64, False),
    (64, 64, False),
    (128, 64, False),
    (192, 64, False),
    (256, 192, True),
    (448, 96, False),
    (544, 96, False),
    (640, 192, True),
)
SUMS = dict(
    L=(640, 192), V=(448, 192), U=(256, 192), M=(192, 64), N=(64, 64), R=(128, 64), O=(0, 64)
)


class Plan:
    def __init__(self, direct):
        self.direct = direct
        self.shape = (4, 2) if direct else (1, 1)
        self.count = self.shape[0] * self.shape[1]
        self.rows = PACKED_ROWS if direct else STARTS[8]
        self.offsets = {}
        for name, start, width in zip(NAMES, STARTS, WIDTHS):
            self.offsets[name] = (
                PACKED[name] if direct else start,
                width // self.count,
            )

    def load(self, ref, name):
        start, size = self.offsets[name]
        return ref[:, :, start : start + size, :].reshape(self.count * size, D)

    def store(self, ref, name, value):
        start, size = self.offsets[name]
        ref[:, :, start : start + size, :] = value.astype(ref.dtype).reshape(*self.shape, size, D)


    def store_part(self, ref, name, i, value):
        start, size = self.offsets[name]
        if self.direct:
            ref[i, :, start : start + size, :] = value.astype(ref.dtype).reshape(2, size, D)
        else:
            ref[0, 0, start + i * D : start + (i + 1) * D, :] = value.astype(ref.dtype)


class Mail:
    def __init__(self, send_sems, recv_sems):
        self.sems = (send_sems, recv_sems)
        self.table = {}

    def add(self, key, source, target, device):
        index = len(self.table)

        def build():
            return pltpu.make_async_remote_copy(
                src_ref=source(),
                dst_ref=target(),
                send_sem=self.sems[0].at[index],
                recv_sem=self.sems[1].at[index],
                device_id=device,
                device_id_type=MESH,
            )

        self.table[key] = build

    def start(self, *keys):
        for key in keys:
            self.table[key]().start()

    def wait(self, *keys):
        for key in keys:
            self.table[key]().wait_recv()

    def close(self):
        for build in self.table.values():
            build().wait_send()


MESSAGES = 150


def aligned(start, size):
    return pl.ds(pl.multiple_of(start, 16), size)


def step_kernel(plan, names, *refs):
    r = SimpleNamespace(**dict(zip(names, refs)))
    dp = lax.axis_index("dp")
    pipe = lax.axis_index("pipe")
    slot, half = pipe // 2, lax.rem(pipe, 2)
    y, c = slot, half
    z, x = dp // 2, lax.rem(dp, 2)
    mail = Mail(r.send_sems, r.recv_sems)
    wts, grads, gains = r.wts, r.grads, r.gains

    def at(z_to, x_to, y_to, c_to):
        return {"dp": z_to * 2 + x_to, "pipe": y_to * 2 + c_to}

    partner = {"pipe": pipe + 1 - 2 * half}
    rings = [lax.rem(z + k, 4) for k in (1, 2, 3)]
    plane = [(1 - x, y), (x, 1 - y), (1 - x, 1 - y)]
    mates = [(1 - y, c), (y, 1 - c), (1 - y, 1 - c)]

    barrier = pltpu.get_barrier_semaphore()
    if plan.direct:
        peers = [at(to, x, y, c) for to in rings]
        peers += [at(z, tx, ty, c) for tx, ty in plane]
        peers += [at(z, x, y, 1 - c), at(z, x, 1 - y, 1 - c)]
        peers += [at(to, 1 - x, y, c) for to in rings]
    else:
        peers = [partner]
    for peer in peers:
        pl.semaphore_signal(barrier, inc=1, device_id=peer, device_id_type=MESH)

    loads = {}
    local_sems = r.local_sems

    def load(key, source, target):
        loads[key] = pltpu.make_async_copy(source, target, local_sems.at[len(loads)])
        loads[key].start()

    if plan.direct:
        at_row = 0
        for name, width in zip(NAMES, WIDTHS):
            size = width // SHARDS
            load(
                "w" + name,
                r.master.at[pl.ds(at_row, size), :],
                r.h1.at[pl.ds(PACKED[name], size), :],
            )
            at_row += size
    else:
        load("w", r.weights_in, wts.at[0, 0])
    source, raw = r.pool.at[pl.ds(0, 1920), :], r.raw
    tokens = raw.shape[0]
    for i, (name, ref) in enumerate((("noise", r.noise), ("single", r.single), ("state", r.state))):
        load(name, ref.at[slot], source.at[pl.ds(0, tokens), pl.ds(i * PIN, PIN)])
    load("double", r.double.at[slot], raw)

    allh, everyone = r.allh, r.everyone
    base = pl.multiple_of(half * ROWS, 16)
    mail.add(
        "h2",
        lambda: allh.at[aligned(half * ROWS, 864), :],
        lambda: allh.at[aligned(half * ROWS, 864), :],
        partner,
    )
    mail.add(
        "dh2",
        lambda: everyone.at[pl.ds(base, ROWS), :],
        lambda: everyone.at[pl.ds(base, ROWS), :],
        partner,
    )
    if plan.direct:

        def same(key, view, device):
            mail.add(key, view, view, device)

        own = []
        for g, (start, rows, quartered) in enumerate(GATHERS):
            size = rows // 4 if quartered else rows // 2
            mine = aligned(start + (2 * y + c if quartered else c) * size, size)
            other = aligned(start + (2 * (1 - y) + c) * size, size)
            own.append(mine)
            for k, to in enumerate(rings):
                same(f"gz{g}{k}", lambda mine=mine: wts.at[z, x, mine, :], at(to, x, y, c))
            same(f"gx{g}", lambda mine=mine: wts.at[:, x, mine, :], at(z, 1 - x, y, c))
            if quartered:
                same(f"gy{g}", lambda mine=mine: wts.at[:, :, mine, :], at(z, x, 1 - y, c))
                same(f"gc{g}", lambda mine=mine: wts.at[:, :, mine, :], at(z, x, y, 1 - c))
                same(f"gd{g}", lambda other=other: wts.at[:, :, other, :], at(z, x, y, 1 - c))
            else:
                same(f"gc{g}", lambda mine=mine: wts.at[:, x, mine, :], at(z, x, y, 1 - c))
                same(f"gd{g}", lambda mine=mine: wts.at[:, 1 - x, mine, :], at(z, x, y, 1 - c))
        tot, tot_z, tot_x = r.tot, r.tot_z, r.tot_x
        for k, to in enumerate(rings):
            mail.add(f"tz{k}", lambda: tot_z.at[z], lambda: tot_z.at[z], at(to, x, y, c))
        mail.add("tx", lambda: tot, lambda: tot_x, at(z, 1 - x, y, c))
        pair_in, plane_in, ring_out, ring_in, final = (
            r.pair_in, r.plane_in, r.ring_out, r.ring_in, r.final,
        )
        for key, (start, rows) in SUMS.items():
            h, q = rows // 2, rows // 4
            away = aligned(start + (1 - c) * h, h)
            mail.add(
                key + "c",
                lambda away=away: grads.at[:, :, away, :],
                lambda start=start, h=h: pair_in.at[:, :, pl.ds(start // 2, h), :],
                at(z, x, y, 1 - c),
            )
            for k, (tx, ty) in enumerate(plane):
                piece = aligned(start + c * h + ty * q, q)
                mail.add(
                    f"{key}p{k}",
                    lambda tx=tx, piece=piece: grads.at[:, tx, piece, :],
                    lambda k=k, start=start, q=q: plane_in.at[k, :, pl.ds(start // 4, q), :],
                    at(z, tx, ty, c),
                )
            for k, to in enumerate(rings):
                mail.add(
                    f"{key}z{k}",
                    lambda to=to, start=start, q=q: ring_out.at[to, pl.ds(start // 4, q), :],
                    lambda start=start, q=q: ring_in.at[z, pl.ds(start // 4, q), :],
                    at(to, x, y, c),
                )
            done = aligned(start + c * h + y * q, q)
            for k, (ty, tc) in enumerate(mates):
                same(f"{key}g{k}", lambda done=done: final.at[done, :], at(z, x, ty, tc))
        small, small_c, small_p, small_z = r.small, r.small_c, r.small_p, r.small_z
        mail.add("sc", lambda: small.at[0], lambda: small_c, at(z, x, y, 1 - c))
        for k, (tx, ty) in enumerate(plane):
            mail.add(f"sp{k}", lambda: small.at[1], lambda k=k: small_p.at[k], at(z, tx, ty, c))
        for k, to in enumerate(rings):
            mail.add(f"sz{k}", lambda: small_z.at[z], lambda: small_z.at[z], at(to, x, y, c))
        square = r.square
        for k in range(1, SHARDS):
            to = lax.rem(dp + k, SHARDS)
            mail.add(
                f"n{k}",
                lambda: square.at[dp],
                lambda: square.at[dp],
                {"dp": to, "pipe": pipe},
            )

    def sum_pair(key):
        start, rows = SUMS[key]
        h = rows // 2
        mail.wait(key + "c")
        keep = aligned(start + c * h, h)
        for i in range(4):
            grads[i, :, keep, :] = (
                grads[i, :, keep, :].astype(F32)
                + pair_in[i, :, start // 2 : start // 2 + h, :].astype(F32)
            ).astype(BF16)
        mail.start(*(f"{key}p{k}" for k in range(3)))

    def sum_plane(key):
        start, rows = SUMS[key]
        h, q = rows // 2, rows // 4
        mail.wait(*(f"{key}p{k}" for k in range(3)))
        keep = aligned(start + c * h + y * q, q)
        spot = slice(start // 4, start // 4 + q)
        total = grads[:, x, keep, :].astype(F32)
        for k in range(3):
            total = total + plane_in[k, :, spot, :].astype(F32)
        ring_out[:, spot, :] = total.astype(BF16)
        ring_in[z, spot, :] = ring_out[z, spot, :]
        mail.start(*(f"{key}z{k}" for k in range(3)))

    def sum_ring(key):
        start, rows = SUMS[key]
        h, q = rows // 2, rows // 4
        mail.wait(*(f"{key}z{k}" for k in range(3)))
        spot = slice(start // 4, start // 4 + q)
        total = ring_in[0, spot, :].astype(F32)
        for k in range(1, 4):
            total = total + ring_in[k, spot, :].astype(F32)
        final[aligned(start + c * h + y * q, q), :] = total.astype(BF16)
        mail.start(*(f"{key}g{k}" for k in range(3)))

    def gather_z(g):
        mail.start(*(f"gz{g}{k}" for k in range(3)))

    def gather_x(g):
        mail.wait(*(f"gz{g}{k}" for k in range(3)))
        if GATHERS[g][2]:
            mail.start(f"gx{g}")
        else:
            mail.start(f"gx{g}", f"gc{g}")

    def gather_y(g):
        mail.wait(f"gx{g}")
        if GATHERS[g][2]:
            mail.start(f"gy{g}", f"gc{g}")
        else:
            mail.start(f"gd{g}")

    def gather_core(g):
        mail.wait(f"gy{g}")
        mail.start(f"gd{g}")

    def gathered(*groups):
        for g in groups:
            mail.wait(f"gc{g}", f"gd{g}")

    def steps(*pairs):
        def run():
            for function, value in pairs:
                function(value)

        return run

    def pump(index, *stages):
        if plan.direct:
            for k, stage in enumerate(stages):
                if stage is not None:
                    pl.when(index == k)(stage)

    def direct(function, *values):
        if plan.direct:
            function(*values)

    lat = jnp.zeros(r.lat_row.shape, F32)
    columns = lat.shape[1]
    for j in range(LATN):
        lat = jnp.where(r.lat_row[...] == j, r.lat_weight[j].astype(F32), lat)
    live = jnp.concatenate(
        [jnp.full((1, columns), r.live[0, i], jnp.int32) for i in range(lat.shape[0])], axis=0
    )
    if plan.direct:
        summed = jnp.zeros(lat.shape, F32)
        for lev in range(LEV):
            token = lax.broadcasted_iota(jnp.int32, lat.shape, 1) + lev * columns
            weigh = r.lev_weight[lev].astype(F32) * lat * 1e-06
            summed = summed + jnp.where(token < live, weigh, 0.0)
        summed = jnp.sum(jnp.sum(summed, axis=1, keepdims=True), axis=0, keepdims=True)
        tot_z[z] = jnp.broadcast_to(summed, (8, LANES))
    pl.semaphore_wait(barrier, len(peers))
    if plan.direct:
        mail.start("tz0", "tz1", "tz2")
        for name in NAMES:
            loads["w" + name].wait()
        r.h1[SPARE, :] = jnp.zeros((16, D), F32)
        for g, mine in enumerate(own):
            wts[z, x, mine, :] = r.h1[mine, :].astype(BF16)
            if g < 2:
                gather_z(g)

    order_row, order_col = r.order_row, r.order_col
    order_row[...] = jnp.full(order_row.shape, -1, jnp.int32)
    order_row[:, :tokens] = jnp.where(slot > 0, r.order[1:2, :], r.order[0:1, :])
    order_col[...] = column_of(order_row[...]).astype(jnp.int32)
    table = column_of(r.table[...]).astype(jnp.int32)
    column = r.column
    column[...] = jnp.where(table >= 0, table + 8 * half, -9)
    lat_own = jnp.where(slot > 0, lat[1:2, :], lat[0:1, :])
    lat_col = r.lat_col
    lat_col[...] = column_of(
        jnp.concatenate([lat_own, jnp.zeros((1, lat_col.shape[0] - columns), F32)], axis=1)
    )
    live_own = jnp.full((1, LANES), r.live[0, slot], jnp.int32)
    ftime = r.ftime[0, slot]
    pick_double = r.flag[0, slot].astype(F32)
    token_w, velocity = r.dh1.at[:, pl.ds(0, PIN)], r.dh1.at[:, pl.ds(PIN, PIN)]
    for name in ("noise", "single", "double", "state"):
        loads[name].wait()
    picks, joined = r.picks, r.joined
    second = jnp.full((1, PIN), pick_double, F32).astype(BF16)
    first = jnp.full((1, PIN), 1.0 - pick_double, F32).astype(BF16)
    source[tokens:, :] = jnp.zeros((source.shape[0] - tokens, D), BF16)
    source[:tokens, PIN : 2 * PIN] = source[:tokens, PIN : 2 * PIN] * first + raw[...] * second
    lane = lax.broadcasted_iota(jnp.int32, (1, LANES), 1)
    direct(steps((gather_x, 0), (gather_z, 2)))

    @pl.loop(0, TILES)
    def _(t):
        rows = tile_at(t)
        spots = order_col[aligned(half * 864 + t * TILE, TILE), :]
        for b in range(1920 // LANES):
            picks[:, b * LANES : (b + 1) * LANES] = jnp.where(
                spots == lane + b * LANES, 1.0, 0.0
            ).astype(BF16)
        drawn = dot(picks[:, :1920], source[...])
        noisy = (1.0 - ftime) * drawn[:, 0:PIN] + ftime * drawn[:, PIN : 2 * PIN]
        joined[rows, 0:PIN] = noisy.astype(BF16)
        joined[rows, PIN:] = drawn[:, 2 * PIN :].astype(BF16)
        pump(
            t,
            steps((gather_x, 1), (gather_z, 3)),
            steps((gather_x, 2), (gather_z, 4)),
            steps((gather_y, 0)),
        )

    if plan.direct:
        mail.wait("tz0", "tz1", "tz2")
        tot[...] = ((tot_z[0] + tot_z[1]) + tot_z[2]) + tot_z[3]
        mail.start("tx")

    @pl.loop(0, CHUNKS)
    def _(k):
        for lev in range(LEV):
            spot = pl.ds(pl.multiple_of(lev * WSZ + k * 16, 16), 16)
            rows = pl.ds(pl.multiple_of(k * CROWS + lev * 8, 8), 8)
            speed = source[spot, PIN : 2 * PIN].astype(F32) - source[spot, 0:PIN].astype(F32)
            velocity[rows, :] = jnp.where(half > 0, speed[8:16], speed[0:8])
            weigh = (
                r.lev_weight[lev].astype(F32)
                * lat_col[pl.ds(pl.multiple_of(k * 16 + half * 8, 8), 8), :]
                * 1e-06
            )
            token_w[rows, :] = jnp.where(column[rows, :] < live_own, weigh, 0.0)
        rows = pl.ds(pl.multiple_of(k * CROWS + LEV * 8, 8), 8)
        velocity[rows, :] = jnp.zeros((8, PIN), F32)
        token_w[rows, :] = jnp.zeros((8, LANES), F32)

    if plan.direct:
        gather_y(1)
        gather_x(3)
        gather_z(5)

    @pl.loop(0, TILES)
    def _(t):
        rows = tile_at(t)
        spots = column[rows, :]
        for b in range(1920 // LANES):
            value = jnp.where(
                spots == order_row[:, b * LANES : (b + 1) * LANES], 1.0, 0.0
            ).astype(BF16)
            if b < HEADS:
                r.probs2[rows, head_lanes(b)] = value
            else:
                r.ctx2[rows, head_lanes(b - HEADS)] = value
        pump(t, steps((gather_y, 2)))

    if plan.direct:
        mail.wait("tx")
        r.scale[...] = 1.0 / (PIN * (tot[...] + r.tot_x[...]))
        gathered(0, 1, 2)
    else:
        r.scale[...] = jnp.broadcast_to(r.scale_in[0:1, :], (8, LANES))
        loads["w"].wait()

    h0, a_s, r1, ctx1 = r.h0, r.a, r.r1, r.ctx1
    probs1, h1, m_s, slope, y_s = r.probs1, r.h1, r.m, r.slope, r.y

    @pl.loop(0, TILES)
    def _(t):
        rows = tile_at(t)
        low = (dot(joined[rows, :], plan.load(wts, "E")) + ftime * gains[4:5, :]).astype(BF16)
        h0[rows, :] = low
        scaled, _ = standardize(low.astype(F32))
        normed = (scaled * gains[0:1, :]).astype(BF16)
        a_s[rows, :] = normed
        r1[rows, :] = dot_nt(normed, plan.load(wts, "A1")).astype(BF16)
        pump(
            t,
            steps((gather_x, 4), (gather_z, 6)),
            None,
            steps((gather_x, 5), (gather_z, 7), (gather_y, 3)),
        )

    def window(w):
        starts = [w * WSZ + start for start in (0, LANES, 0)]
        if not isinstance(w, int):
            starts = [pl.multiple_of(start, 16) for start in starts]
        return (w, *(pl.ds(start, size) for start, size in zip(starts, (LANES, TAIL, WSZ))))

    @pl.loop(0, WINS)
    def _(w):
        attend_windows(r1, [window(w)], probs1, r.probs1_tail, ctx1, {})
        pump(
            w,
            None,
            None,
            None,
            steps((gather_x, 6), (gather_y, 4)),
            None,
            None,
            steps((gather_y, 5), (gather_x, 7), (gather_core, 4), (gather_y, 6)),
        )

    direct(gathered, 3, 4)

    @pl.loop(0, TILES)
    def _(t):
        rows = tile_at(t)
        mixed = h0[rows, :].astype(F32) + dot(ctx1[rows, :], plan.load(wts, "O1"))
        h1[rows, :] = mixed
        scaled, _ = standardize(mixed)
        normed = (scaled * gains[1:2, :]).astype(BF16)
        m_s[rows, :] = normed
        upper = dot_nt(normed, plan.load(wts, "U"))
        coef = 0.7978845608028654
        square = upper * upper
        bent = jnp.tanh(coef * (upper + 0.044715 * (square * upper)))
        half_up = 0.5 * (1.0 + bent)
        y_s[rows, :] = (upper * half_up).astype(BF16)
        slope[rows, :] = (
            half_up
            + 0.5 * upper * (1.0 - bent * bent) * (coef * (1.0 + 3 * 0.044715 * square))
        ).astype(BF16)
        pump(t, None, steps((gather_y, 7)))

    direct(gathered, 5, 6)

    @pl.loop(0, TILES)
    def _(t):
        rows = tile_at(t)
        allh[aligned(half * 864 + t * TILE, TILE), :] = (
            h1[rows, :] + dot(y_s[rows, :], plan.load(wts, "V"))
        ).astype(BF16)

    mail.start("h2")
    allh[13 * WSZ :, :] = jnp.zeros((allh.shape[0] - 13 * WSZ, D), BF16)
    small_own = small.at[0] if plan.direct else r.tail
    small_own[...] = jnp.zeros((8, D), F32)
    direct(gather_core, 7)
    mail.wait("h2")

    tiles = [pl.ds(t * TILE, TILE) for t in range(TILES)]
    h2, c_s = r.pool.at[pl.ds(0, ROWS), :], r.pool.at[pl.ds(ROWS, ROWS), :]
    r2, ctx2, dctx = r.r2, r.ctx2, r.dctx
    probs2, dh3_s, f_s, dpred_s, dr2 = r.probs2, r.dh3, r.f, r.dpred, r2
    scale = r.scale[0:1, :]

    for rows in tiles:
        drawn = dot(probs2[rows, :], allh[:FF, :]) + dot(ctx2[rows, :], allh[FF:, :])
        h2[rows, :] = drawn.astype(BF16)

    direct(gathered, 7)

    for t, rows in enumerate(tiles):
        scaled, _ = standardize(h2[rows, :].astype(F32))
        normed = (scaled * gains[2:3, :]).astype(BF16)
        c_s[rows, :] = normed
        r2[rows, :] = dot_nt(normed, plan.load(wts, "A2")).astype(BF16)

    def chunks(k):
        return [
            pl.ds(pl.multiple_of((k * 3 + part) * CROWS, 16), CROWS) for part in range(3)
        ]

    key = lax.broadcasted_iota(jnp.int32, (CROWS, LANES), 0)
    ask = lax.broadcasted_iota(jnp.int32, (CROWS, LANES), 1)
    keep = (lax.bitwise_and(key, 7) == lax.bitwise_and(ask, 7)) & (key < LEV * 8)
    r.bias[...] = jnp.where(keep, 0.0, -1e30)
    @pl.loop(0, 3)
    def _(k):
        attend_columns(r2, chunks(k), probs2, r.bias[...], ctx2)

    for t, rows in enumerate(tiles):
        o2 = plan.load(wts, "O2")
        deq = plan.load(wts, "Q")
        hidden = (h2[rows, :].astype(F32) + dot(ctx2[rows, :], o2)).astype(BF16).astype(F32)
        scaled, spread = standardize(hidden)
        normed = (scaled * gains[3:4, :]).astype(BF16)
        f_s[rows, :] = normed
        error = dot_nt(normed, deq) - velocity[rows, :]
        weighed = token_w[rows, :] * error
        small_own[5:6, 0:PIN] += jnp.sum(weighed * error, axis=0, keepdims=True) * scale
        dpred = (2.0 * scale * weighed).astype(BF16)
        dpred_s[rows, :] = dpred
        upstream = dot(dpred, deq)
        small_own[3:4, :] += jnp.sum(upstream * scaled, axis=0, keepdims=True)
        dh3 = standardize_back(scaled, spread, gains[3:4, :], upstream).astype(BF16)
        dh3_s[rows, :] = dh3
        dctx[rows, :] = dot_nt(dh3, o2).astype(BF16)

    plan.store(grads, "Q", dot_tn(dpred_s[...], f_s[...]))
    plan.store(grads, "O2", dot_tn(ctx2[...], dh3_s[...]))

    @pl.loop(0, 3)
    def _(k):
        attend_columns_back(r2, chunks(k), probs2, dctx)

    plan.store(grads, "A2", dot_tn(dr2[...], c_s[...]))
    direct(mail.start, "Lc")

    for t, rows in enumerate(tiles):
        upstream = dot(dr2[rows, :], plan.load(wts, "A2"))
        scaled, spread = standardize(h2[rows, :].astype(F32))
        small_own[2:3, :] += jnp.sum(upstream * scaled, axis=0, keepdims=True)
        back = standardize_back(scaled, spread, gains[2:3, :], upstream)
        everyone[aligned(base + t * TILE, TILE), :] = (
            dh3_s[rows, :].astype(F32) + back
        ).astype(BF16)

    mail.start("dh2")
    everyone[2 * ROWS :, :] = jnp.zeros((everyone.shape[0] - 2 * ROWS, D), BF16)
    direct(sum_pair, "L")
    mail.wait("dh2")

    dh2_s, do_s, dh0_s, dr1, du_s, dh1_s = c_s, f_s, dh3_s, r1, slope, r.dh1

    @pl.loop(0, TILES)
    def _(t):
        rows = tile_at(t)
        spots = order_col[aligned(half * 864 + t * TILE, TILE), :]
        row = lax.broadcasted_iota(jnp.int32, (TILE, LANES), 0) + t * TILE
        spots = jnp.where(row < WSZ * half, -1, spots)
        for b in range(2048 // LANES):
            picks[:, b * LANES : (b + 1) * LANES] = jnp.where(
                spots == r.both[:, b * LANES : (b + 1) * LANES], 1.0, 0.0
            ).astype(BF16)
        dh2_s[rows, :] = dot(picks[...], everyone[...]).astype(BF16)

    for i in range(4):
        part = slice(i * D, (i + 1) * D)
        plan.store_part(grads, "V", i, dot_tn(y_s[:, part], dh2_s[...]))
    direct(mail.start, "Vc")

    @pl.loop(0, TILES)
    def _(t):
        rows = tile_at(t)
        low = dh2_s[rows, :]
        du = (dot_nt(low, plan.load(wts, "V")) * slope[rows, :].astype(F32)).astype(BF16)
        du_s[rows, :] = du
        upstream = dot(du, plan.load(wts, "U"))
        scaled, spread = standardize(h1[rows, :])
        small_own[1:2, :] += jnp.sum(upstream * scaled, axis=0, keepdims=True)
        dh1 = low.astype(F32) + standardize_back(scaled, spread, gains[1:2, :], upstream)
        dh1_s[rows, :] = dh1
        do = dh1.astype(BF16)
        do_s[rows, :] = do
        dctx[rows, :] = dot_nt(do, plan.load(wts, "O1")).astype(BF16)
        pump(t, steps((sum_pair, "V")), None, steps((sum_plane, "L")))

    for i in range(4):
        part = slice(i * D, (i + 1) * D)
        plan.store_part(grads, "U", i, dot_tn(du_s[:, part], m_s[...]))
    direct(mail.start, "Uc")
    plan.store(grads, "O1", dot_tn(ctx1[...], do_s[...]))
    direct(mail.start, "Mc")

    @pl.loop(0, WINS)
    def _(w):
        attend_windows_back(r1, [window(w)], probs1, r.probs1_tail, dctx, {})
        pump(
            w,
            None,
            steps((sum_pair, "U"), (sum_pair, "M"), (sum_ring, "L")),
            None,
            None,
            steps((sum_plane, "V")),
        )

    plan.store(grads, "A1", dot_tn(dr1[...], a_s[...]))
    direct(mail.start, "Nc", "Rc")
    direct(steps((sum_plane, "U"), (sum_ring, "V")))

    @pl.loop(0, TILES)
    def _(t):
        rows = tile_at(t)
        upstream = dot(dr1[rows, :], plan.load(wts, "A1"))
        scaled, spread = standardize(h0[rows, :].astype(F32))
        small_own[0:1, :] += jnp.sum(upstream * scaled, axis=0, keepdims=True)
        back = standardize_back(scaled, spread, gains[0:1, :], upstream)
        dh0 = (dh1_s[rows, :] + back).astype(BF16)
        dh0_s[rows, :] = dh0
        small_own[4:5, :] += ftime * jnp.sum(dh0.astype(F32), axis=0, keepdims=True)
        pump(
            t,
            None,
            steps((sum_pair, "N"), (sum_pair, "R"), (sum_plane, "M")),
            steps((sum_ring, "U"), (sum_ring, "M")),
        )

    plan.store(grads, "E", dot_tn(joined[...], dh0_s[...]))
    if not plan.direct:
        out = pltpu.make_async_copy(grads.at[0, 0], r.grads_out, local_sems.at[15])
        out.start()
        out.wait()
        mail.close()
        return

    grads[:, :, SPARE, :] = jnp.zeros((4, 2, 16, D), BF16)
    mail.start("Oc", "sc")
    sum_plane("N")
    mail.wait("sc")
    small[1] = small[0] + small_c[...]
    mail.start("sp0", "sp1", "sp2")
    sum_pair("O")
    sum_plane("R")
    sum_ring("N")

    def hand_out(squares, names):
        for name in names:
            number = NAMES.index(name)
            spot, size = STARTS[number] // SHARDS, WIDTHS[number] // SHARDS
            part = final[PACKED[name] : PACKED[name] + size, :]
            r.total[spot : spot + size, :] = part
            part = part.astype(F32)
            squares = squares + jnp.sum((part * part).reshape(size // 16, 16, D), axis=0)
        return squares

    for key in ("L", "V", "U", "M"):
        mail.wait(*(f"{key}g{k}" for k in range(3)))
    squares = hand_out(jnp.zeros((16, D), F32), NAMES[2:])
    mail.wait("sp0", "sp1", "sp2")
    small_z[z] = (small[1] + small_p[0]) + (small_p[1] + small_p[2])
    mail.start("sz0", "sz1", "sz2")
    sum_plane("O")
    sum_ring("R")
    mail.wait("sz0", "sz1", "sz2")
    r.tail[...] = ((small_z[0] + small_z[1]) + small_z[2]) + small_z[3]
    sum_ring("O")
    for key in ("N", "R", "O"):
        mail.wait(*(f"{key}g{k}" for k in range(3)))
    squares = hand_out(squares, NAMES[:2])
    norm = jnp.sum(jnp.sum(squares, axis=1, keepdims=True), axis=0, keepdims=True)
    square[dp] = jnp.broadcast_to(norm, (8, LANES))
    mail.start(*(f"n{k}" for k in range(1, SHARDS)))
    mail.wait(*(f"n{k}" for k in range(1, SHARDS)))
    norm = square[0]
    for k in range(1, SHARDS):
        norm = norm + square[k]
    r.norm[...] = norm
    mail.close()


def adam_update(param, grad, first, second, average, correction, decay_rate, rate):
    first_new = BETA * first + (1.0 - BETA) * grad
    second_new = BETA * second + (1.0 - BETA) * grad * grad
    direction = first_new * correction / (jnp.sqrt(second_new * correction) + EPS_ADAM)
    param_new = param - rate * (direction + decay_rate * param)
    average_new = EMA_RATE * average + (1.0 - EMA_RATE) * param_new
    return (param_new, first_new, second_new, average_new)


def update_kernel(
    step, tail, norm, total, master, first, second, average, gains, gain_first, gain_second, gain_average,
    loss_out, norm_out, new_w, new_f, new_s, new_a, low, new_g, new_gf, new_gs, new_ga,
    held, made, made_low, in_sems, out_sems,
):
    rows = made_low.shape[1]

    def fetch(i, k):
        source = (master, first, second, average)[k].at[pl.ds(i * rows, rows), :]
        return pltpu.make_async_copy(source, held.at[i, k], in_sems.at[i, k])

    def give(i, k):
        target = (new_w, new_f, new_s, new_a, low)[k].at[pl.ds(i * rows, rows), :]
        source = made_low.at[i] if k == 4 else made.at[i, k]
        return pltpu.make_async_copy(source, target, out_sems.at[i, k])

    pieces = held.shape[0]
    for i in range(pieces):
        for k in range(4):
            fetch(i, k).start()
    gain_grad = tail[0:5, :]
    square = jnp.sum(jnp.sum(gain_grad * gain_grad, axis=1, keepdims=True), axis=0, keepdims=True)
    size = jnp.sqrt(norm[0:1, 0:1] + square)
    factor = jnp.minimum(1.0, CLIP_MAX / (size + 1e-06))
    steps = jnp.full((1, 1), step[0].astype(F32), F32)
    correction = 1.0 / (1.0 - jnp.exp2(-steps))
    for i in range(pieces):
        for k in range(4):
            fetch(i, k).wait()
        results = adam_update(
            held[i, 0], factor * total[i * rows : (i + 1) * rows, :].astype(F32),
            held[i, 1], held[i, 2], held[i, 3], correction, DECAY_WEIGHT, RATE,
        )
        for k, value in enumerate(results):
            made[i, k] = value
        made_low[i] = results[0].astype(BF16)
        for k in range(5):
            give(i, k).start()
    norm_out[...] = size
    loss_out[...] = jnp.sum(tail[5:6, 0:PIN], axis=1, keepdims=True)
    results = adam_update(
        gains[...], factor * gain_grad, gain_first[...], gain_second[...], gain_average[...],
        correction, 0.0, GAIN_RATE,
    )
    for ref, value in zip((new_g, new_gf, new_gs, new_ga), results):
        ref[...] = value
    for i in range(pieces):
        for k in range(5):
            give(i, k).wait()


def column_table():
    row = np.arange(1024)
    chunk, inner = row // CROWS, row % CROWS
    level, col = inner // 8, inner % 8
    token = level * WSZ + chunk * 16 + col
    return np.where((row < ROWS) & (level < LEV), token, -9).astype(np.int32)


def shape_of(rows, columns, dtype):
    return jax.ShapeDtypeStruct((rows, columns), dtype)


def local(
    noise_draw, single_step, double_step, state_now, target_flag, flow_time, live_count,
    latitude_row, window_order, latitude_weight, level_weight, step_count,
    master_weights, first_moment, second_moment, average_weights,
    gain_rows, gain_first, gain_second, gain_average,
):
    micro = noise_draw.shape[0]
    tokens = noise_draw.shape[1]
    members = lax.axis_size("dp")
    plan = Plan(members == SHARDS)
    smem = pl.BlockSpec(memory_space=pltpu.SMEM)
    vmem = pl.BlockSpec(memory_space=pltpu.VMEM)
    anym = pl.BlockSpec(memory_space=pl.ANY)
    table = column_table()
    both = np.full((2048,), -8, np.int32)
    for h in range(2):
        both[h * ROWS : (h + 1) * ROWS] = np.where(table[:ROWS] >= 0, table[:ROWS] + 8 * h, -8)

    inputs = dict(
        noise=(noise_draw, anym),
        single=(single_step, anym),
        double=(double_step, anym),
        state=(state_now, anym),
        flag=(target_flag.T, smem),
        ftime=(flow_time.T, smem),
        live=(live_count.T, smem),
        lat_row=(latitude_row, vmem),
        order=(window_order, vmem),
        lat_weight=(latitude_weight, smem),
        lev_weight=(level_weight, smem),
        gains=(gain_rows, vmem),
        table=(jnp.asarray(table)[None, :], vmem),
        both=(jnp.asarray(both)[None, :], vmem),
    )
    if plan.direct:
        inputs |= dict(master=(master_weights, anym))
        outputs = dict(
            total=(shape_of(master_weights.shape[0], D, BF16), vmem),
            tail=(shape_of(8, D, F32), vmem),
            norm=(shape_of(8, LANES, F32), vmem),
        )
    else:
        gathered = lax.all_gather(master_weights.astype(BF16), "dp", axis=0, tiled=True)
        inputs |= dict(weights_in=(natural_order(gathered, members), anym))
        lat_match = latitude_row[:, :, None] == jnp.arange(LATN, dtype=jnp.int32)[None, None, :]
        lat_values = jnp.sum(
            jnp.where(lat_match, latitude_weight.astype(F32)[None, None, :], 0.0), axis=2
        )
        weigh = (level_weight.astype(F32)[None, :, None] * lat_values[:, None, :]).reshape(
            micro, tokens
        ) * 1e-06
        alive = jnp.arange(tokens, dtype=jnp.int32)[None, :] < live_count
        total = lax.psum(jnp.sum(jnp.where(alive, weigh, 0.0)), "dp")
        inputs |= dict(scale_in=(jnp.full((8, LANES), 1.0 / (PIN * total), F32), vmem))
        outputs = dict(
            grads_out=(shape_of(plan.rows, D, BF16), anym),
            tail=(shape_of(8, D, F32), vmem),
        )
    scratch = dict(
        wts=pltpu.VMEM((*plan.shape, plan.rows, D), BF16),
        grads=pltpu.VMEM((*plan.shape, plan.rows, D), BF16),
        raw=pltpu.VMEM((tokens, PIN), BF16),
        pool=pltpu.VMEM((2 * ROWS, D), BF16),
        picks=pltpu.VMEM((TILE, 2048), BF16),
        order_row=pltpu.VMEM((1, 1920), jnp.int32),
        order_col=pltpu.VMEM((1920, LANES), jnp.int32),
        column=pltpu.VMEM((1024, LANES), jnp.int32),
        lat_col=pltpu.VMEM((256, LANES), F32),
        scale=pltpu.VMEM((8, LANES), F32),
        joined=pltpu.VMEM((ROWS, 2 * PIN), BF16),
        h0=pltpu.VMEM((ROWS, D), BF16),
        a=pltpu.VMEM((ROWS, D), BF16),
        r1=pltpu.VMEM((ROWS, 3 * D), BF16),
        probs1=pltpu.VMEM((WINS, WSZ, HEADS * LANES), BF16),
        probs1_tail=pltpu.VMEM((WINS, WSZ, HEADS * TAIL), BF16),
        bias=pltpu.VMEM((CROWS, LANES), F32),
        ctx1=pltpu.VMEM((ROWS, D), BF16),
        h1=pltpu.VMEM((ROWS, D), F32),
        m=pltpu.VMEM((ROWS, D), BF16),
        slope=pltpu.VMEM((ROWS, FF), BF16),
        y=pltpu.VMEM((ROWS, FF), BF16),
        allh=pltpu.VMEM((1920, D), BF16),
        r2=pltpu.VMEM((ROWS, 3 * D), BF16),
        probs2=pltpu.VMEM((ROWS, HEADS * LANES), BF16),
        ctx2=pltpu.VMEM((ROWS, D), BF16),
        dctx=pltpu.VMEM((ROWS, D), BF16),
        dh3=pltpu.VMEM((ROWS, D), BF16),
        f=pltpu.VMEM((ROWS, D), BF16),
        dpred=pltpu.VMEM((ROWS, PIN), BF16),
        everyone=pltpu.VMEM((2048, D), BF16),
        dh1=pltpu.VMEM((ROWS, D), F32),
        local_sems=pltpu.SemaphoreType.DMA((16,)),
        send_sems=pltpu.SemaphoreType.DMA((MESSAGES if plan.direct else 2,)),
        recv_sems=pltpu.SemaphoreType.DMA((MESSAGES if plan.direct else 2,)),
    )
    if plan.direct:
        scratch |= dict(
            tot=pltpu.VMEM((8, LANES), F32),
            tot_z=pltpu.VMEM((4, 8, LANES), F32),
            tot_x=pltpu.VMEM((8, LANES), F32),
            pair_in=pltpu.VMEM((4, 2, PACKED_ROWS // 2, D), BF16),
            plane_in=pltpu.VMEM((3, 4, PACKED_ROWS // 4, D), BF16),
            ring_out=pltpu.VMEM((4, PACKED_ROWS // 4, D), BF16),
            ring_in=pltpu.VMEM((4, PACKED_ROWS // 4, D), BF16),
            final=pltpu.VMEM((PACKED_ROWS, D), BF16),
            small=pltpu.VMEM((2, 8, D), F32),
            small_c=pltpu.VMEM((8, D), F32),
            small_p=pltpu.VMEM((3, 8, D), F32),
            small_z=pltpu.VMEM((4, 8, D), F32),
            square=pltpu.VMEM((SHARDS, 8, LANES), F32),
        )
    names = [*inputs, *outputs, *scratch]
    results = pl.pallas_call(
        functools.partial(step_kernel, plan, names),
        out_shape=[value[0] for value in outputs.values()],
        in_specs=[value[1] for value in inputs.values()],
        out_specs=[value[1] for value in outputs.values()],
        scratch_shapes=list(scratch.values()),
        compiler_params=pltpu.CompilerParams(
            vmem_limit_bytes=VMEM_MAX, collective_id=0, has_side_effects=True
        ),
        name="train_step",
    )(*(value[0] for value in inputs.values()))
    results = SimpleNamespace(**dict(zip(outputs, results)))
    if plan.direct:
        total, tail, norm = results.total, results.tail, results.norm
    else:
        grads = stored_order(results.grads_out.astype(F32), members)
        total = lax.psum_scatter(grads, "dp", scatter_dimension=0, tiled=True)
        total, tail = lax.psum(total, "pipe"), lax.psum(results.tail, ("dp", "pipe"))
        norm = jnp.full((8, LANES), lax.psum(jnp.sum(total * total), "dp"), F32)
    shard = master_weights.shape[0]
    pieces = 3 if shard % 48 == 0 else 1
    block = shard // pieces
    outs = pl.pallas_call(
        update_kernel,
        out_shape=[shape_of(1, 1, F32)] * 2
        + [shape_of(shard, D, F32)] * 4
        + [shape_of(shard, D, BF16)]
        + [shape_of(5, D, F32)] * 4,
        in_specs=[smem] + [vmem] * 3 + [anym] * 4 + [vmem] * 4,
        out_specs=[vmem] * 2 + [anym] * 5 + [vmem] * 4,
        scratch_shapes=[
            pltpu.VMEM((pieces, 4, block, D), F32),
            pltpu.VMEM((pieces, 4, block, D), F32),
            pltpu.VMEM((pieces, block, D), BF16),
            pltpu.SemaphoreType.DMA((pieces, 4)),
            pltpu.SemaphoreType.DMA((pieces, 5)),
        ],
        compiler_params=pltpu.CompilerParams(vmem_limit_bytes=VMEM_MAX),
        name="update",
    )(
        step_count, tail, norm, total, master_weights, first_moment, second_moment, average_weights,
        gain_rows, gain_first, gain_second, gain_average,
    )
    return (outs[0][0, 0], outs[1][0, 0], *outs[2:])


def solution(mesh):
    over = P("dp", None)
    token = P(None, "dp", None)
    pair = P(None, "dp")
    in_specs = (token,) * 4 + (pair,) * 5 + (P(),) * 3 + (over,) * 4 + (P(),) * 4
    out_specs = (P(), P()) + (over,) * 5 + (P(),) * 4
    return jax.shard_map(local, mesh=mesh, in_specs=in_specs, out_specs=out_specs, check_vma=False)
```

profile of v0, /device:TPU:0, one launch (start us, length us, event | category | flops | bytes accessed | tf_op | source)
XLA Modules:
  0.0 134.4 jit_solution(10921754585769571983)
XLA Ops:
  1.3 126.4 %train_step.1 = (bf16[816,384]{1,0:T(8,128)(2,1)}, f32[8,384]{1,0:T(8,128)}, f32[8,128]{1,0:T(8,128)}) custom-call(bf16[2,1872,128]{2,1,0:T(8,128)(2,1)} %refs_0_.1, bf16[2,1872,128]{2,1,0:T(8,128)(2,1)} %refs_1_.1, bf16[2,1872,128]{2,1,0:T(8,128)(2,1)} %refs_2_.1, bf16[2,1872,128]{2,1,0:T(8,128)(2,1)} %refs_3_.1, s32[1,2]{1,0:T(1,128)} %bitcast.5, ...), custom_call_target="tpu_custom_call" | custom-call | tf_op jit(solution)/shard_map/train_step/pallas_call | solution.py:1216
  127.7 6.5 %update.1 = (f32[1,1]{1,0:T(1,128)}, f32[1,1]{1,0:T(1,128)}, f32[816,384]{1,0:T(8,128)}, f32[816,384]{1,0:T(8,128)}, f32[816,384]{1,0:T(8,128)}, /*index=5*/f32[...) custom-call(s32[1]{0:T(128)S(6)} %copy.33.step, ...), custom_call_target="tpu_custom_call" | custom-call | tf_op jit(solution)/shard_map/update/pallas_call | solution.py:1238
where the time goes:
time: 135 us; the launch traced here: 134 us
  Pallas kernels  133 us (99%)
  between operations  1.48 us (1%)
    pallas_call x1, Pallas kernels, local(): pl.pallas_call(functools.partial(step_kernel, plan, names), out_shape=[va...  126 us
    pallas_call x1, Pallas kernels, local(): pl.pallas_call(update_kernel, out_shape=[shape_of(1, 1, F32)] * 2 + [shap...  6.46 us

commit v1 on v0

--- a/solution.py
+++ b/solution.py
@@ -408,6 +408,7 @@
 
 
 MESSAGES = 150
+RELAYED = ("L", "V", "U", "M")
 
 
 def aligned(start, size):
@@ -476,12 +477,14 @@
         lambda: allh.at[aligned(half * ROWS, 864), :],
         partner,
     )
-    mail.add(
-        "dh2",
-        lambda: everyone.at[pl.ds(base, ROWS), :],
-        lambda: everyone.at[pl.ds(base, ROWS), :],
-        partner,
-    )
+    for t in range(TILES):
+        part = aligned(base + t * TILE, TILE)
+        mail.add(
+            f"dh2{t}",
+            lambda part=part: everyone.at[part, :],
+            lambda part=part: everyone.at[part, :],
+            partner,
+        )
     if plan.direct:
 
         def same(key, view, device):
@@ -536,6 +539,8 @@
                 )
             done = aligned(start + c * h + y * q, q)
             for k, (ty, tc) in enumerate(mates):
+                if k == 2 and key in RELAYED:
+                    done, ty = aligned(start + c * h + (1 - y) * q, q), y
                 same(f"{key}g{k}", lambda done=done: final.at[done, :], at(z, x, ty, tc))
         small, small_c, small_p, small_z = r.small, r.small_c, r.small_p, r.small_z
         mail.add("sc", lambda: small.at[0], lambda: small_c, at(z, x, y, 1 - c))
@@ -587,7 +592,11 @@
         for k in range(1, 4):
             total = total + ring_in[k, spot, :].astype(F32)
         final[aligned(start + c * h + y * q, q), :] = total.astype(BF16)
-        mail.start(*(f"{key}g{k}" for k in range(3)))
+        mail.start(*(f"{key}g{k}" for k in range(2 if key in RELAYED else 3)))
+
+    def sum_relay(key):
+        mail.wait(key + "g0")
+        mail.start(key + "g2")
 
     def gather_z(g):
         mail.start(*(f"gz{g}{k}" for k in range(3)))
@@ -895,11 +904,11 @@
         everyone[aligned(base + t * TILE, TILE), :] = (
             dh3_s[rows, :].astype(F32) + back
         ).astype(BF16)
-
-    mail.start("dh2")
+        mail.start(f"dh2{t}")
+
     everyone[2 * ROWS :, :] = jnp.zeros((everyone.shape[0] - 2 * ROWS, D), BF16)
     direct(sum_pair, "L")
-    mail.wait("dh2")
+    mail.wait("dh20", "dh21", "dh22")
 
     dh2_s, do_s, dh0_s, dr1, du_s, dh1_s = c_s, f_s, dh3_s, r1, slope, r.dh1
 
@@ -991,6 +1000,8 @@
     small[1] = small[0] + small_c[...]
     mail.start("sp0", "sp1", "sp2")
     sum_pair("O")
+    for key in RELAYED:
+        sum_relay(key)
     sum_plane("R")
     sum_ring("N")
 
@@ -1004,8 +1015,8 @@
             squares = squares + jnp.sum((part * part).reshape(size // 16, 16, D), axis=0)
         return squares
 
-    for key in ("L", "V", "U", "M"):
-        mail.wait(*(f"{key}g{k}" for k in range(3)))
+    for key in RELAYED:
+        mail.wait(key + "g1", key + "g2")
     squares = hand_out(jnp.zeros((16, D), F32), NAMES[2:])
     mail.wait("sp0", "sp1", "sp2")
     small_z[z] = (small[1] + small_p[0]) + (small_p[1] + small_p[2])
@@ -1041,13 +1052,14 @@
 def update_kernel(
     step, tail, norm, total, master, first, second, average, gains, gain_first, gain_second, gain_average,
     loss_out, norm_out, new_w, new_f, new_s, new_a, low, new_g, new_gf, new_gs, new_ga,
-    held, made, made_low, in_sems, out_sems,
+    held, held_grad, made, made_low, in_sems, out_sems,
 ):
     rows = made_low.shape[1]
 
     def fetch(i, k):
-        source = (master, first, second, average)[k].at[pl.ds(i * rows, rows), :]
-        return pltpu.make_async_copy(source, held.at[i, k], in_sems.at[i, k])
+        source = (master, first, second, average, total)[k].at[pl.ds(i * rows, rows), :]
+        target = held_grad.at[i] if k == 4 else held.at[i, k]
+        return pltpu.make_async_copy(source, target, in_sems.at[i, k])
 
     def give(i, k):
         target = (new_w, new_f, new_s, new_a, low)[k].at[pl.ds(i * rows, rows), :]
@@ -1056,7 +1068,7 @@
 
     pieces = held.shape[0]
     for i in range(pieces):
-        for k in range(4):
+        for k in range(5):
             fetch(i, k).start()
     gain_grad = tail[0:5, :]
     square = jnp.sum(jnp.sum(gain_grad * gain_grad, axis=1, keepdims=True), axis=0, keepdims=True)
@@ -1065,10 +1077,10 @@
     steps = jnp.full((1, 1), step[0].astype(F32), F32)
     correction = 1.0 / (1.0 - jnp.exp2(-steps))
     for i in range(pieces):
-        for k in range(4):
+        for k in range(5):
             fetch(i, k).wait()
         results = adam_update(
-            held[i, 0], factor * total[i * rows : (i + 1) * rows, :].astype(F32),
+            held[i, 0], factor * held_grad[i].astype(F32),
             held[i, 1], held[i, 2], held[i, 3], correction, DECAY_WEIGHT, RATE,
         )
         for k, value in enumerate(results):
@@ -1193,8 +1205,8 @@
         everyone=pltpu.VMEM((2048, D), BF16),
         dh1=pltpu.VMEM((ROWS, D), F32),
         local_sems=pltpu.SemaphoreType.DMA((16,)),
-        send_sems=pltpu.SemaphoreType.DMA((MESSAGES if plan.direct else 2,)),
-        recv_sems=pltpu.SemaphoreType.DMA((MESSAGES if plan.direct else 2,)),
+        send_sems=pltpu.SemaphoreType.DMA((MESSAGES if plan.direct else 4,)),
+        recv_sems=pltpu.SemaphoreType.DMA((MESSAGES if plan.direct else 4,)),
     )
     if plan.direct:
         scratch |= dict(
@@ -1241,13 +1253,14 @@
         + [shape_of(shard, D, F32)] * 4
         + [shape_of(shard, D, BF16)]
         + [shape_of(5, D, F32)] * 4,
-        in_specs=[smem] + [vmem] * 3 + [anym] * 4 + [vmem] * 4,
+        in_specs=[smem] + [vmem] * 2 + [anym] * 5 + [vmem] * 4,
         out_specs=[vmem] * 2 + [anym] * 5 + [vmem] * 4,
         scratch_shapes=[
             pltpu.VMEM((pieces, 4, block, D), F32),
+            pltpu.VMEM((pieces, block, D), total.dtype),
             pltpu.VMEM((pieces, 4, block, D), F32),
             pltpu.VMEM((pieces, block, D), BF16),
-            pltpu.SemaphoreType.DMA((pieces, 4)),
+            pltpu.SemaphoreType.DMA((pieces, 5)),
             pltpu.SemaphoreType.DMA((pieces, 5)),
         ],
         compiler_params=pltpu.CompilerParams(vmem_limit_bytes=VMEM_MAX),

time: 135 us -> 133 us (0.985)
  no operation moved by 1% of the time
where the time goes in v1:
time: 133 us
  Pallas kernels  132 us (99%)
  between operations  1.48 us (1%)
    pallas_call x1, Pallas kernels, local(): pl.pallas_call(functools.partial(step_kernel, plan, names), out_shape=[va...  126 us
    pallas_call x1, Pallas kernels, local(): pl.pallas_call(update_kernel, out_shape=[shape_of(1, 1, F32)] * 2 + [shap...  6.15 us

profile of v1, /device:TPU:0, one launch (start us, length us, event | category | flops | bytes accessed | tf_op | source)
XLA Modules:
  0.0 133.2 jit_solution(6995510011013648553)
XLA Ops:
  1.3 125.6 %train_step.1 = (bf16[816,384]{1,0:T(8,128)(2,1)}, f32[8,384]{1,0:T(8,128)}, f32[8,128]{1,0:T(8,128)}) custom-call(bf16[2,1872,128]{2,1,0:T(8,128)(2,1)} %refs_0_.1, bf16[2,1872,128]{2,1,0:T(8,128)(2,1)} %refs_1_.1, bf16[2,1872,128]{2,1,0:T(8,128)(2,1)} %refs_2_.1, bf16[2,1872,128]{2,1,0:T(8,128)(2,1)} %refs_3_.1, s32[1,2]{1,0:T(1,128)} %bitcast.5, ...), custom_call_target="tpu_custom_call" | custom-call | tf_op jit(solution)/shard_map/train_step/pallas_call | solution.py:1228
  126.9 6.2 %update.1 = (f32[1,1]{1,0:T(1,128)}, f32[1,1]{1,0:T(1,128)}, f32[816,384]{1,0:T(8,128)}, f32[816,384]{1,0:T(8,128)}, f32[816,384]{1,0:T(8,128)}, /*index=5*/f32[...) custom-call(s32[1]{0:T(128)S(6)} %copy.33.step, ...), custom_call_target="tpu_custom_call" | custom-call | tf_op jit(solution)/shard_map/update/pallas_call | solution.py:1250

commit v2 on v1

--- a/solution.py
+++ b/solution.py
@@ -471,12 +471,11 @@
 
     allh, everyone = r.allh, r.everyone
     base = pl.multiple_of(half * ROWS, 16)
-    mail.add(
-        "h2",
-        lambda: allh.at[aligned(half * ROWS, 864), :],
-        lambda: allh.at[aligned(half * ROWS, 864), :],
-        partner,
-    )
+    for k, (start, size) in enumerate(((0, 528), (528, 336))):
+        part = aligned(half * ROWS + start, size)
+        mail.add(
+            f"h2{k}", lambda part=part: allh.at[part, :], lambda part=part: allh.at[part, :], partner
+        )
     for t in range(TILES):
         part = aligned(base + t * TILE, TILE)
         mail.add(
@@ -823,19 +822,19 @@
 
     direct(gathered, 5, 6)
 
-    @pl.loop(0, TILES)
-    def _(t):
-        rows = tile_at(t)
+    for t in range(TILES):
+        rows = pl.ds(t * TILE, TILE)
         allh[aligned(half * 864 + t * TILE, TILE), :] = (
             h1[rows, :] + dot(y_s[rows, :], plan.load(wts, "V"))
         ).astype(BF16)
-
-    mail.start("h2")
+        if t > 0:
+            mail.start(f"h2{t - 1}")
+
     allh[13 * WSZ :, :] = jnp.zeros((allh.shape[0] - 13 * WSZ, D), BF16)
     small_own = small.at[0] if plan.direct else r.tail
     small_own[...] = jnp.zeros((8, D), F32)
     direct(gather_core, 7)
-    mail.wait("h2")
+    mail.wait("h20", "h21")
 
     tiles = [pl.ds(t * TILE, TILE) for t in range(TILES)]
     h2, c_s = r.pool.at[pl.ds(0, ROWS), :], r.pool.at[pl.ds(ROWS, ROWS), :]
@@ -1205,8 +1204,8 @@
         everyone=pltpu.VMEM((2048, D), BF16),
         dh1=pltpu.VMEM((ROWS, D), F32),
         local_sems=pltpu.SemaphoreType.DMA((16,)),
-        send_sems=pltpu.SemaphoreType.DMA((MESSAGES if plan.direct else 4,)),
-        recv_sems=pltpu.SemaphoreType.DMA((MESSAGES if plan.direct else 4,)),
+        send_sems=pltpu.SemaphoreType.DMA((MESSAGES if plan.direct else 5,)),
+        recv_sems=pltpu.SemaphoreType.DMA((MESSAGES if plan.direct else 5,)),
     )
     if plan.direct:
         scratch |= dict(

time: 133 us -> 133 us (level)
  no operation moved by 1% of the time
where the time goes in v2:
time: 133 us
  Pallas kernels  132 us (99%)
  between operations  1.48 us (1%)
    pallas_call x1, Pallas kernels, local(): pl.pallas_call(functools.partial(step_kernel, plan, names), out_shape=[va...  125 us
    pallas_call x1, Pallas kernels, local(): pl.pallas_call(update_kernel, out_shape=[shape_of(1, 1, F32)] * 2 + [shap...  6.15 us

profile of v2, /device:TPU:0, one launch (start us, length us, event | category | flops | bytes accessed | tf_op | source)
XLA Modules:
  0.0 133.1 jit_solution(14614564594380785977)
XLA Ops:
  1.3 125.4 %train_step.1 = (bf16[816,384]{1,0:T(8,128)(2,1)}, f32[8,384]{1,0:T(8,128)}, f32[8,128]{1,0:T(8,128)}) custom-call(bf16[2,1872,128]{2,1,0:T(8,128)(2,1)} %refs_0_.1, bf16[2,1872,128]{2,1,0:T(8,128)(2,1)} %refs_1_.1, bf16[2,1872,128]{2,1,0:T(8,128)(2,1)} %refs_2_.1, bf16[2,1872,128]{2,1,0:T(8,128)(2,1)} %refs_3_.1, s32[1,2]{1,0:T(1,128)} %bitcast.5, ...), custom_call_target="tpu_custom_call" | custom-call | tf_op jit(solution)/shard_map/train_step/pallas_call | solution.py:1227
  126.7 6.2 %update.1 = (f32[1,1]{1,0:T(1,128)}, f32[1,1]{1,0:T(1,128)}, f32[816,384]{1,0:T(8,128)}, f32[816,384]{1,0:T(8,128)}, f32[816,384]{1,0:T(8,128)}, /*index=5*/f32[...) custom-call(s32[1]{0:T(128)S(6)} %copy.33.step, ...), custom_call_target="tpu_custom_call" | custom-call | tf_op jit(solution)/shard_map/update/pallas_call | solution.py:1249
